TPU v7x, 128 devices: a whole 4x4x4 slice. The times are simulated.
128 devices in a mesh: dp: 16 (over x, z_hi, core), head: 8 (over z_lo, y).
Axes of the slice: x: 4, y: 4, z: 4 (z_hi: 2, z_lo: 2; z = z_hi * 2 + z_lo), core: 2. Of those that a mesh axis runs over, the one named last changes fastest.
Arguments:
- latent: bfloat16 [16384, 512], P(('dp', 'head')), may hold values from -32 to 32
- out_grad: bfloat16 [16384, 16, 8, 256], P('dp', None, 'head'), may hold values from -6 to 6
- weight: float32 [512, 16, 8, 256], P(None, 'dp', 'head'), may hold values from -0.25 to 0.25
- moment_one: float32 [512, 16, 8, 256], P(None, 'dp', 'head'), may hold values from -4 to 4
- moment_two: float32 [512, 16, 8, 256], P(None, 'dp', 'head'), may hold values from 0.1 to 2
Outputs:
- latent_grad: bfloat16 [16384, 512], P(('dp', 'head'))
- new_weight: float32 [512, 16, 8, 256], P(None, 'dp', 'head')
- new_moment_one: float32 [512, 16, 8, 256], P(None, 'dp', 'head')
- new_moment_two: float32 [512, 16, 8, 256], P(None, 'dp', 'head')
All inputs are finite; a program needn't handle non-finite values.
Results may differ from a plain program's by a relative error of at most 0.014.
Values may be sent and summed in bfloat16 or wider, within the bound.
No kernel may reach another device: no remote copies, remote signals or barrier semaphores. Data moves between devices by JAX's collectives and lax.ppermute only.
A program may use at most 128 MiB of HBM per device.

v0:
```python
import math
import jax
import jax.numpy as jnp
from jax import lax
from jax.sharding import PartitionSpec as P


def sent_to_all(x, axis):
    peers = lax.axis_size(axis)
    return lax.all_to_all(jnp.broadcast_to(x[None], (peers, *x.shape)), axis, 0, 0, tiled=True)


def laid_out(tiles, dim):
    tiles = jnp.moveaxis(tiles, 0, dim)
    dims = tiles.shape
    return tiles.reshape(*dims[:dim], dims[dim] * dims[dim + 1], *dims[dim + 2 :])


def gathered_copies(x, axis, dim):
    tiles = sent_to_all(x, axis)
    return laid_out(tiles, dim)


def in_blocks(x, dim, peers):
    dims = x.shape
    tiles = x.reshape(*dims[:dim], peers, dims[dim] // peers, *dims[dim + 1 :])
    return jnp.moveaxis(tiles, dim, 0)


def summed_on_arrival(x, axis, dim):
    tiles = in_blocks(x, dim, lax.axis_size(axis))
    arrived = lax.all_to_all(tiles, axis, split_axis=0, concat_axis=0, tiled=True)
    return arrived.astype(jnp.float32).sum(axis=0)


def hadamard(length):
    row_index = jnp.arange(length, dtype=jnp.int32)[:, None]
    col_index = jnp.arange(length, dtype=jnp.int32)[None, :]
    common = jnp.bitwise_and(row_index, col_index)
    parity = jnp.zeros((length, length), jnp.int32)
    for position in range(length.bit_length()):
        parity = parity + jnp.bitwise_and(jnp.right_shift(common, position), 1)
    sign_table = 1.0 - 2.0 * jnp.bitwise_and(parity, 1).astype(jnp.float32)
    return sign_table / math.sqrt(length)


def local(latent, out_grad, weight, moment_one, moment_two):
    dp_count = lax.axis_size("dp")
    latent_width = latent.shape[1]
    rotation = hadamard(latent_width)
    gathered = gathered_copies(latent, "head", 0)
    tokens_all = gathered.shape[0] * dp_count
    weight_half = weight.astype(jnp.bfloat16)
    grads_block = out_grad
    partial_value = jnp.einsum(
        "tahc,lahc->tl",
        grads_block,
        lax.all_gather(weight_half, "dp", axis=1, tiled=True),
        preferred_element_type=jnp.float32,
    )
    latent_grad = summed_on_arrival(partial_value.astype(jnp.bfloat16), "head", 0).astype(
        jnp.bfloat16
    )
    grads_block = out_grad
    partial_value = jnp.einsum(
        "tl,tahc->alc", gathered, grads_block, preferred_element_type=jnp.float32
    )
    rotated = jnp.einsum("ml,alc->amc", rotation, partial_value)
    spread = jnp.sqrt(jnp.mean(rotated * rotated, axis=1, keepdims=True) + 1e-06)
    outgoing = jnp.clip(rotated, -2.0 * spread, 2.0 * spread).astype(jnp.bfloat16)
    received = lax.all_to_all(outgoing, "dp", split_axis=0, concat_axis=0, tiled=True)
    summed = jnp.sum(received.astype(jnp.float32), axis=0)
    gradient = jnp.dot(rotation, summed) * tokens_all ** (-0.5)
    gradient = gradient.reshape(weight.shape)
    new_moment_one = 0.9 * moment_one + 0.1 * gradient
    new_moment_two = 0.95 * moment_two + 0.05 * gradient * gradient
    update = (
        new_moment_one / (1.0 - 0.9**10) / (jnp.sqrt(new_moment_two / (1.0 - 0.95**10)) + 1e-08)
    )
    new_weight = weight - 0.001 * (update + 0.1 * weight)
    return (latent_grad, new_weight, new_moment_one, new_moment_two)


def solution(mesh):
    placed = (
        P(("dp", "head"), None),
        P("dp", None, "head", None),
        P(None, "dp", "head", None),
        P(None, "dp", "head", None),
        P(None, "dp", "head", None),
    )
    return jax.shard_map(
        local,
        mesh=mesh,
        in_specs=placed,
        out_specs=(
            P(("dp", "head"), None),
            P(None, "dp", "head", None),
            P(None, "dp", "head", None),
            P(None, "dp", "head", None),
        ),
        check_vma=False,
    )
```

profile of v0, /device:TPU:1, one launch (start us, length us, event | category | flops | bytes accessed | tf_op | source)
XLA Modules:
  0.0 149.6 jit_solution(12734567798015555913)
XLA Ops:
  7.2 0.0 all-gather.2.cloned.1.call-start
  7.2 1.8 %copy.36 = bf16[512,1,1,256]{3,0,2,1:T(8,128)(2,1)} copy(f32[512,1,1,256]{3,2,1,0:T(1,128)} %param.7) | data formatting | bytes 786432 | tf_op args[2]
  9.0 0.0 all-gather.2.cloned.1.call-update
  9.0 2.0 %broadcast_in_dim.2 = bf16[8,128,512]{2,1,0:T(8,128)(2,1)} broadcast(bf16[128,512]{1,0:T(8,128)(2,1)} %param.5), dimensions={1,2} | broadcast | bytes 1179648 | tf_op jit(solution)/shard_map/broadcast_in_dim | solution.py:10
  11.0 6.4 %all-to-all-start.1 = ((bf16[8,128,512]{2,1,0:T(8,128)(2,1)}), bf16[8,128,512]{2,1,0:T(8,128)(2,1)S(1)}, u32[]{:S(2)}, u32[]{:S(2)}) async-start(bf16[8,128,512]{2,1,0:T(8,128)(2,1)} %broadcast_in_dim.2), calls=%async_computation.1 | async-start | bytes 2097152 | tf_op jit(solution)/shard_map/all_to_all | solution.py:10
  17.4 12.3 %copy.27 = bf16[1024,16,256]{0,2,1:T(8,128)(2,1)} copy(bf16[1024,16,256]{2,1,0:T(8,128)(2,1)} %bitcast.34) | data formatting | bytes 16777216 | tf_op jit(solution)/shard_map/reshape.1
  29.7 3.7 %all-to-all-done.1 = bf16[8,128,512]{2,1,0:T(8,128)(2,1)S(1)} async-done(((bf16[8,128,512]{2,1,0:T(8,128)(2,1)}), bf16[8,128,512]{2,1,0:T(8,128)(2,1)S(1)}, u32[]{:S(2)}, u32[]{:S(2)}) %all-to-all-start.1) | async-done | bytes 1048608 | tf_op jit(solution)/shard_map/all_to_all | solution.py:10
  33.4 12.4 %multiply_reduce_fusion = (f32[16,256]{1,0:T(8,128)S(1)}, bf16[16,256,512]{2,1,0:T(8,128)(2,1)}) fusion(bf16[1024,16,256]{0,2,1:T(8,128)(2,1)} %copy.27, bf16[1024,512,1]{1,0,2:T(8,128)(2,1)S(1)} %bitcast.35), kind=kOutput, calls=%fused_computation.4 | convolution fusion | flops 6457913344 | bytes 13647872 | tf_op jit(solution)/shard_map/ml,alc->amc/dot_general | solution.py:68
  45.8 4.2 %fusion.2 = bf16[16,512,256]{1,2,0:T(8,128)(2,1)} fusion(bf16[16,256,512]{2,1,0:T(8,128)(2,1)} %get-tuple-element.18, bf16[16,256]{1,0:T(8,128)(2,1)S(1)} %get-tuple-element.16, bf16[16,256]{1,0:T(8,128)(2,1)S(1)} %get-tuple-element.15), kind=kLoop, calls=%fused_computation.5 | loop fusion | flops 4194304 | bytes 8404992 | tf_op jit(solution)/shard_map/convert_element_type | solution.py:70
  49.9 8.2 %all-to-all-start.2 = ((bf16[16,512,256]{1,2,0:T(8,128)(2,1)}), bf16[16,512,256]{1,2,0:T(8,128)(2,1)}, u32[]{:S(2)}, u32[]{:S(2)}) async-start(bf16[16,512,256]{1,2,0:T(8,128)(2,1)} %fusion.2), calls=%async_computation.2 | async-start | bytes 8388608 | tf_op jit(solution)/shard_map/all_to_all | solution.py:71
  58.1 43.2 %all-gather.2.cloned.1.call-done = bf16[512,16,1,256]{3,0,2,1:T(8,128)(2,1)} async-done(((bf16[512,1,1,256]{3,0,2,1:T(8,128)(2,1)}), bf16[512,16,1,256]{3,0,2,1:T(8,128)(2,1)}) %all-gather.2.cloned.1.call-update) | async-done | bytes 4194320 | tf_op jit(solution)/shard_map/all_gather | solution.py:58
  101.3 10.1 %bitcast_convert_fusion = bf16[1024,512]{1,0:T(8,128)(2,1)} fusion(bf16[1024,16,256]{0,2,1:T(8,128)(2,1)} %copy.27, bf16[512,16,1,256]{3,0,2,1:T(8,128)(2,1)} %all-gather.2.cloned.1.call-done), kind=kOutput, calls=%fused_computation.8 | convolution fusion | flops 4295491584 | bytes 13631488 | tf_op jit(solution)/shard_map/tahc,lahc->tl/dot_general | solution.py:55
  111.4 0.0 copy-start
  111.4 0.0 copy-start.1
  111.4 0.0 copy-start.2
  111.4 4.1 %all-to-all-done.2 = bf16[16,512,256]{1,2,0:T(8,128)(2,1)} async-done(((bf16[16,512,256]{1,2,0:T(8,128)(2,1)}), bf16[16,512,256]{1,2,0:T(8,128)(2,1)}, u32[]{:S(2)}, u32[]{:S(2)}) %all-to-all-start.2) | async-done | bytes 4194336 | tf_op jit(solution)/shard_map/all_to_all | solution.py:71
  115.5 10.6 %all-to-all-start = ((bf16[8,128,512]{2,1,0:T(8,128)(2,1)}), bf16[8,128,512]{2,1,0:T(8,128)(2,1)S(1)}, u32[]{:S(2)}, u32[]{:S(2)}) async-start(bf16[8,128,512]{2,1,0:T(8,128)(2,1)} %bitcast.3), calls=%async_computation | async-start | bytes 2097152 | tf_op jit(solution)/shard_map/all_to_all | solution.py:32
  126.0 2.7 %convert_reduce_fusion = bf16[512,256]{0,1:T(8,128)(2,1)S(1)} fusion(bf16[16,512,256]{1,2,0:T(8,128)(2,1)} %all-to-all-done.2), kind=kLoop, calls=%fused_computation.2 | loop fusion | flops 4063232 | bytes 4456448 | tf_op jit(solution)/shard_map/reduce_sum | solution.py:72
  128.8 0.0 copy-done
  128.8 0.0 copy-done.1
  128.8 0.0 copy-done.2
  128.8 1.7 %multiply_subtract_fusion = (f32[512,1,1,256]{3,0,2,1:T(8,128)S(1)}, f32[512,1,1,256]{3,0,2,1:T(8,128)S(1)}, f32[512,1,1,256]{3,0,2,1:T(8,128)S(1)}) fusion(f32[512,1,1,256]{3,2,1,0:T(1,128)S(1)} %copy-done, f32[512,1,1,256]{3,2,1,0:T(1,128)S(1)} %copy-done.1, f32[512,1,1,256]{3,2,1,0:T(1,128)S(1)} %copy-done.2, bf16[512,256]{0,1:T(8,128)(2,1)S(1)} %convert_reduce_fusion), kind=kOutput, calls=%fused_computation.16 | convolution fusion | flops 145489920 | bytes 3407872 | tf_op jit(solution)/shard_map/dot_general | solution.py:73
  130.5 1.3 copy.24
  131.9 1.3 copy.25
  133.2 1.3 copy.26
  134.5 7.4 %all-to-all-done = bf16[8,128,512]{2,1,0:T(8,128)(2,1)S(1)} async-done(((bf16[8,128,512]{2,1,0:T(8,128)(2,1)}), bf16[8,128,512]{2,1,0:T(8,128)(2,1)S(1)}, u32[]{:S(2)}, u32[]{:S(2)}) %all-to-all-start) | async-done | bytes 1048608 | tf_op jit(solution)/shard_map/all_to_all | solution.py:32
  141.9 0.8 reduce_sum.34
  (1 shorter events, 0.0 us)
Async XLA Ops:
  7.2 94.1 %all-gather.2.cloned.1.call-start = ((), (), s32[]{:S(2)}) async-start(), calls=%async_computation.3 | async-start | bytes 4456448 | tf_op jit(solution)/shard_map/all_gather | solution.py:58
  11.0 22.3 %all-to-all-start.1 = ((bf16[8,128,512]{2,1,0:T(8,128)(2,1)}), bf16[8,128,512]{2,1,0:T(8,128)(2,1)S(1)}, u32[]{:S(2)}, u32[]{:S(2)}) async-start(bf16[8,128,512]{2,1,0:T(8,128)(2,1)} %broadcast_in_dim.2), calls=%async_computation.1 | async-start | bytes 2097152 | tf_op jit(solution)/shard_map/all_to_all | solution.py:10
  49.9 65.5 %all-to-all-start.2 = ((bf16[16,512,256]{1,2,0:T(8,128)(2,1)}), bf16[16,512,256]{1,2,0:T(8,128)(2,1)}, u32[]{:S(2)}, u32[]{:S(2)}) async-start(bf16[16,512,256]{1,2,0:T(8,128)(2,1)} %fusion.2), calls=%async_computation.2 | async-start | bytes 8388608 | tf_op jit(solution)/shard_map/all_to_all | solution.py:71
  111.4 17.4 %copy-start = (f32[512,1,1,256]{3,2,1,0:T(1,128)S(1)}, f32[512,1,1,256]{3,2,1,0:T(1,128)}, u32[]{:S(2)}) copy-start(f32[512,1,1,256]{3,2,1,0:T(1,128)} %param.7) | copy-start | bytes 1572868
  111.4 17.4 %copy-start.1 = (f32[512,1,1,256]{3,2,1,0:T(1,128)S(1)}, f32[512,1,1,256]{3,2,1,0:T(1,128)}, u32[]{:S(2)}) copy-start(f32[512,1,1,256]{3,2,1,0:T(1,128)} %param.8) | copy-start | bytes 1572868
  111.4 17.4 %copy-start.2 = (f32[512,1,1,256]{3,2,1,0:T(1,128)S(1)}, f32[512,1,1,256]{3,2,1,0:T(1,128)}, u32[]{:S(2)}) copy-start(f32[512,1,1,256]{3,2,1,0:T(1,128)} %param.9) | copy-start | bytes 1572868
  115.5 26.4 %all-to-all-start = ((bf16[8,128,512]{2,1,0:T(8,128)(2,1)}), bf16[8,128,512]{2,1,0:T(8,128)(2,1)S(1)}, u32[]{:S(2)}, u32[]{:S(2)}) async-start(bf16[8,128,512]{2,1,0:T(8,128)(2,1)} %bitcast.3), calls=%async_computation | async-start | bytes 2097152 | tf_op jit(solution)/shard_map/all_to_all | solution.py:32
Sparse Core Ops, SparseCore 0:
  10.9 90.3 all-gather.1
where the time goes:
time: 150 us
  waiting for transfers between devices  58.3 us (39%)
  starting transfers between devices  25.1 us (17%)
  matrix products  24.1 us (16%)
  local copies, waits for them, and re-layouts  20.1 us (13%)
  between operations  14.1 us (9%)
  other arithmetic  7.77 us (5%)
    all_gather x1, waiting for transfers between devices, local(): lax.all_gather(weight_half, 'dp', axis=1, tiled=True)  43.2 us
    dot_general x1, matrix products, local(): rotated = jnp.einsum('ml,alc->amc', rotation, partial_value)  12.4 us
    another operation x1, local copies, waits for them, and re-layouts  12.3 us
    all_to_all x1, starting transfers between devices, summed_on_arrival(): lax.all_to_all(tiles, axis, split_axis=0, concat_axis=0, tiled=True)  10.6 us
    dot_general x1, matrix products, local(): jnp.einsum('tahc,lahc->tl', grads_block, lax.all_gather(weight_half, 'dp'...  10.1 us
    all_to_all x1, starting transfers between devices, local(): lax.all_to_all(outgoing, 'dp', split_axis=0, concat_axis=0, tiled=True)  8.16 us
    all_to_all x1, waiting for transfers between devices, summed_on_arrival(): lax.all_to_all(tiles, axis, split_axis=0, concat_axis=0, tiled=True)  7.4 us
    all_to_all x1, starting transfers between devices, sent_to_all(): lax.all_to_all(jnp.broadcast_to(x[None], (peers, *x.shape)), axis, 0, 0,...  6.36 us
  transfers between devices with their start and end apart: 4, of which 4 were waited for; matrix products, arithmetic and copies ran while one was open for 33% of the time, Pallas kernels for 0%

commit v1 on v0

--- a/solution.py
+++ b/solution.py
@@ -55,7 +55,12 @@
     partial_value = jnp.einsum(
         "tahc,lahc->tl",
         grads_block,
-        lax.all_gather(weight_half, "dp", axis=1, tiled=True),
+        jnp.concatenate(
+            lax.all_to_all(
+                jnp.stack(lax.axis_size("dp") * [weight_half]), "dp", split_axis=0, concat_axis=0
+            ),
+            axis=1,
+        ),
         preferred_element_type=jnp.float32,
     )
     latent_grad = summed_on_arrival(partial_value.astype(jnp.bfloat16), "head", 0).astype(

time: 150 us -> 181 us (1.21)
  the two profiles are of different devices: /device:TPU:1 before, /device:TPU:68 now
where the time goes in v1:
time: 181 us; the launch traced here: 180 us
  waiting for transfers between devices  102 us (56%)
  matrix products  24.1 us (13%)
  starting transfers between devices  23.7 us (13%)
  local copies, waits for them, and re-layouts  20.6 us (11%)
  other arithmetic  9.14 us (5%)
    all_to_all x1, waiting for transfers between devices, local(): lax.all_to_all(outgoing, 'dp', split_axis=0, concat_axis=0, tiled=True)  49.1 us
    all_to_all x1, waiting for transfers between devices, local(): lax.all_to_all(jnp.stack(lax.axis_size('dp') * [weight_half]), 'dp', spli...  30.5 us
    all_to_all x1, waiting for transfers between devices, sent_to_all(): lax.all_to_all(jnp.broadcast_to(x[None], (peers, *x.shape)), axis, 0, 0,...  14.2 us
    dot_general x1, matrix products, local(): rotated = jnp.einsum('ml,alc->amc', rotation, partial_value)  12.3 us
    another operation x1, local copies, waits for them, and re-layouts  12.3 us
    dot_general x1, matrix products, local(): jnp.einsum('tahc,lahc->tl', grads_block, jnp.concatenate(lax.all_to_all(j...  10.1 us
    all_to_all x1, waiting for transfers between devices, summed_on_arrival(): lax.all_to_all(tiles, axis, split_axis=0, concat_axis=0, tiled=True)  7.87 us
    all_to_all x1, starting transfers between devices, local(): lax.all_to_all(outgoing, 'dp', split_axis=0, concat_axis=0, tiled=True)  7.23 us
  transfers between devices with their start and end apart: 4, of which 4 were waited for; matrix products, arithmetic and copies ran while one was open for 27% of the time, Pallas kernels for 0%

profile of v1, /device:TPU:68, one launch (start us, length us, event | category | flops | bytes accessed | tf_op | source)
XLA Modules:
  0.0 179.9 jit_solution(2255026142876569756)
XLA Ops:
  0.6 2.0 %broadcast_in_dim.2 = bf16[8,128,512]{2,1,0:T(8,128)(2,1)} broadcast(bf16[128,512]{1,0:T(8,128)(2,1)} %param.5), dimensions={1,2} | broadcast | bytes 1179648 | tf_op jit(solution)/shard_map/broadcast_in_dim | solution.py:10
  2.6 5.5 %all-to-all-start.2 = ((bf16[8,128,512]{2,1,0:T(8,128)(2,1)}), bf16[8,128,512]{2,1,0:T(8,128)(2,1)S(1)}, u32[]{:S(2)}, u32[]{:S(2)}) async-start(bf16[8,128,512]{2,1,0:T(8,128)(2,1)} %broadcast_in_dim.2), calls=%async_computation.2 | async-start | bytes 2097152 | tf_op jit(solution)/shard_map/all_to_all | solution.py:10
  8.1 1.4 convert_element_type.25
  9.6 14.2 %all-to-all-done.2 = bf16[8,128,512]{2,1,0:T(8,128)(2,1)S(1)} async-done(((bf16[8,128,512]{2,1,0:T(8,128)(2,1)}), bf16[8,128,512]{2,1,0:T(8,128)(2,1)S(1)}, u32[]{:S(2)}, u32[]{:S(2)}) %all-to-all-start.2) | async-done | bytes 1048608 | tf_op jit(solution)/shard_map/all_to_all | solution.py:10
  23.8 2.3 %stack.2 = bf16[16,512,1,1,256]{4,1,3,2,0:T(8,128)(2,1)} broadcast(bf16[512,256]{1,0:T(8,128)(2,1)S(1)} %bitcast.42), dimensions={1,4} | broadcast | bytes 4456448 | tf_op jit(solution)/shard_map/stack | solution.py:60
  26.2 7.2 %all-to-all-start = ((bf16[16,512,1,1,256]{4,1,3,2,0:T(8,128)(2,1)}), bf16[16,512,1,1,256]{4,1,3,2,0:T(8,128)(2,1)}, u32[]{:S(2)}, u32[]{:S(2)}) async-start(bf16[16,512,1,1,256]{4,1,3,2,0:T(8,128)(2,1)} %stack.2), calls=%async_computation | async-start | bytes 8388608 | tf_op jit(solution)/shard_map/all_to_all | solution.py:59
  33.4 12.3 %copy.26 = bf16[1024,16,256]{0,2,1:T(8,128)(2,1)} copy(bf16[1024,16,256]{2,1,0:T(8,128)(2,1)} %bitcast.41) | data formatting | bytes 16777216 | tf_op jit(solution)/shard_map/reshape.2
  45.6 12.3 %multiply_reduce_fusion = (f32[16,256]{1,0:T(8,128)S(1)}, bf16[16,256,512]{2,1,0:T(8,128)(2,1)}) fusion(bf16[1024,16,256]{0,2,1:T(8,128)(2,1)} %copy.26, bf16[1024,512,1]{1,0,2:T(8,128)(2,1)S(1)} %bitcast.43), kind=kOutput, calls=%fused_computation.4 | convolution fusion | flops 6457913344 | bytes 13647872 | tf_op jit(solution)/shard_map/ml,alc->amc/dot_general | solution.py:73
  57.9 4.2 %fusion.2 = bf16[16,512,256]{1,2,0:T(8,128)(2,1)} fusion(bf16[16,256,512]{2,1,0:T(8,128)(2,1)} %get-tuple-element.18, bf16[16,256]{1,0:T(8,128)(2,1)S(1)} %get-tuple-element.16, bf16[16,256]{1,0:T(8,128)(2,1)S(1)} %get-tuple-element.15), kind=kLoop, calls=%fused_computation.5 | loop fusion | flops 4194304 | bytes 8404992 | tf_op jit(solution)/shard_map/convert_element_type | solution.py:75
  62.1 30.5 %all-to-all-done = bf16[16,512,1,1,256]{4,1,3,2,0:T(8,128)(2,1)} async-done(((bf16[16,512,1,1,256]{4,1,3,2,0:T(8,128)(2,1)}), bf16[16,512,1,1,256]{4,1,3,2,0:T(8,128)(2,1)}, u32[]{:S(2)}, u32[]{:S(2)}) %all-to-all-start) | async-done | bytes 4194336 | tf_op jit(solution)/shard_map/all_to_all | solution.py:59
  92.6 7.2 %all-to-all-start.3 = ((bf16[16,512,256]{1,2,0:T(8,128)(2,1)}), bf16[16,512,256]{1,2,0:T(8,128)(2,1)}, u32[]{:S(2)}, u32[]{:S(2)}) async-start(bf16[16,512,256]{1,2,0:T(8,128)(2,1)} %fusion.2), calls=%async_computation.3 | async-start | bytes 8388608 | tf_op jit(solution)/shard_map/all_to_all | solution.py:76
  99.8 10.1 %bitcast_convert_fusion = bf16[1024,512]{1,0:T(8,128)(2,1)} fusion(bf16[1024,16,256]{0,2,1:T(8,128)(2,1)} %copy.26, bf16[16,512,1,1,256]{4,1,3,2,0:T(8,128)(2,1)} %all-to-all-done), kind=kOutput, calls=%fused_computation.8 | convolution fusion | flops 4295491584 | bytes 13631488 | tf_op jit(solution)/shard_map/tahc,lahc->tl/dot_general | solution.py:55
  109.9 0.0 copy-start
  109.9 0.0 copy-start.1
  109.9 0.0 copy-start.2
  109.9 49.1 %all-to-all-done.3 = bf16[16,512,256]{1,2,0:T(8,128)(2,1)} async-done(((bf16[16,512,256]{1,2,0:T(8,128)(2,1)}), bf16[16,512,256]{1,2,0:T(8,128)(2,1)}, u32[]{:S(2)}, u32[]{:S(2)}) %all-to-all-start.3) | async-done | bytes 4194336 | tf_op jit(solution)/shard_map/all_to_all | solution.py:76
  159.0 3.7 %all-to-all-start.1 = ((bf16[8,128,512]{2,1,0:T(8,128)(2,1)}), bf16[8,128,512]{2,1,0:T(8,128)(2,1)S(1)}, u32[]{:S(2)}, u32[]{:S(2)}) async-start(bf16[8,128,512]{2,1,0:T(8,128)(2,1)} %bitcast.5), calls=%async_computation.1 | async-start | bytes 2097152 | tf_op jit(solution)/shard_map/all_to_all | solution.py:32
  162.7 2.8 %convert_reduce_fusion = bf16[512,256]{0,1:T(8,128)(2,1)S(1)} fusion(bf16[16,512,256]{1,2,0:T(8,128)(2,1)} %all-to-all-done.3), kind=kLoop, calls=%fused_computation.2 | loop fusion | flops 4063232 | bytes 4456448 | tf_op jit(solution)/shard_map/reduce_sum | solution.py:77
  165.5 0.0 copy-done
  165.5 0.0 copy-done.1
  165.5 0.0 copy-done.2
  165.5 1.7 multiply_subtract_fusion
  167.2 1.3 copy.23
  168.5 1.3 copy.24
  169.9 1.3 copy.25
  171.2 7.9 %all-to-all-done.1 = bf16[8,128,512]{2,1,0:T(8,128)(2,1)S(1)} async-done(((bf16[8,128,512]{2,1,0:T(8,128)(2,1)}), bf16[8,128,512]{2,1,0:T(8,128)(2,1)S(1)}, u32[]{:S(2)}, u32[]{:S(2)}) %all-to-all-start.1) | async-done | bytes 1048608 | tf_op jit(solution)/shard_map/all_to_all | solution.py:32
  179.1 0.8 reduce_sum.34
  (2 shorter events, 0.1 us)
Async XLA Ops:
  2.6 21.2 %all-to-all-start.2 = ((bf16[8,128,512]{2,1,0:T(8,128)(2,1)}), bf16[8,128,512]{2,1,0:T(8,128)(2,1)S(1)}, u32[]{:S(2)}, u32[]{:S(2)}) async-start(bf16[8,128,512]{2,1,0:T(8,128)(2,1)} %broadcast_in_dim.2), calls=%async_computation.2 | async-start | bytes 2097152 | tf_op jit(solution)/shard_map/all_to_all | solution.py:10
  26.2 66.4 %all-to-all-start = ((bf16[16,512,1,1,256]{4,1,3,2,0:T(8,128)(2,1)}), bf16[16,512,1,1,256]{4,1,3,2,0:T(8,128)(2,1)}, u32[]{:S(2)}, u32[]{:S(2)}) async-start(bf16[16,512,1,1,256]{4,1,3,2,0:T(8,128)(2,1)} %stack.2), calls=%async_computation | async-start | bytes 8388608 | tf_op jit(solution)/shard_map/all_to_all | solution.py:59
  92.6 66.4 %all-to-all-start.3 = ((bf16[16,512,256]{1,2,0:T(8,128)(2,1)}), bf16[16,512,256]{1,2,0:T(8,128)(2,1)}, u32[]{:S(2)}, u32[]{:S(2)}) async-start(bf16[16,512,256]{1,2,0:T(8,128)(2,1)} %fusion.2), calls=%async_computation.3 | async-start | bytes 8388608 | tf_op jit(solution)/shard_map/all_to_all | solution.py:76
  109.9 55.6 %copy-start = (f32[512,1,1,256]{3,2,1,0:T(1,128)S(1)}, f32[512,1,1,256]{3,2,1,0:T(1,128)}, u32[]{:S(2)}) copy-start(f32[512,1,1,256]{3,2,1,0:T(1,128)} %param.7) | copy-start | bytes 1572868
  109.9 55.6 %copy-start.1 = (f32[512,1,1,256]{3,2,1,0:T(1,128)S(1)}, f32[512,1,1,256]{3,2,1,0:T(1,128)}, u32[]{:S(2)}) copy-start(f32[512,1,1,256]{3,2,1,0:T(1,128)} %param.8) | copy-start | bytes 1572868
  109.9 55.6 %copy-start.2 = (f32[512,1,1,256]{3,2,1,0:T(1,128)S(1)}, f32[512,1,1,256]{3,2,1,0:T(1,128)}, u32[]{:S(2)}) copy-start(f32[512,1,1,256]{3,2,1,0:T(1,128)} %param.9) | copy-start | bytes 1572868
  159.0 20.1 %all-to-all-start.1 = ((bf16[8,128,512]{2,1,0:T(8,128)(2,1)}), bf16[8,128,512]{2,1,0:T(8,128)(2,1)S(1)}, u32[]{:S(2)}, u32[]{:S(2)}) async-start(bf16[8,128,512]{2,1,0:T(8,128)(2,1)} %bitcast.5), calls=%async_computation.1 | async-start | bytes 2097152 | tf_op jit(solution)/shard_map/all_to_all | solution.py:32
